TPU v7x, 32 devices: a whole 2x2x4 slice. The times are simulated.
32 devices in a mesh: groups: 2 (over y), row: 16 (over z, x, core).
Axes of the slice: x: 2, y: 2, z: 4, core: 2. Of those that a mesh axis runs over, the one named last changes fastest.
Arguments:
- layer_input: bfloat16 [8192, 512], P('row', 'groups'), parts along dimension 1, may hold values from -6 to 6
- output_grad: bfloat16 [8192, 512], P('row', 'groups'), parts along dimension 1, may hold values from -1.5 to 1.5
- gate_weight: bfloat16 [28672, 8192], P(('groups', 'row')), parts along dimension 0, may hold values from -0.09375 to 0.09375
- up_weight: bfloat16 [28672, 8192], P(('groups', 'row')), parts along dimension 0, may hold values from -0.09375 to 0.09375
- down_weight: bfloat16 [28672, 8192], P(('groups', 'row')), parts along dimension 0, may hold values from -0.046875 to 0.046875
Outputs:
- input_grad: bfloat16 [8192, 512], P('row', 'groups'), parts along dimension 1
- gate_grad: bfloat16 [28672, 8192], P(('groups', 'row')), parts along dimension 0
- up_grad: bfloat16 [28672, 8192], P(('groups', 'row')), parts along dimension 0
- down_grad: bfloat16 [28672, 8192], P(('groups', 'row')), parts along dimension 0
There are 2 independent parts, one for each index of `groups`. A program takes and returns all parts, laid end to end along the dimension named above; each array names one. Nothing has to cross between parts.
All inputs are finite; a program needn't handle non-finite values.
Results may differ from a plain program's by a relative error of at most 0.0049.
Values may be sent and summed in bfloat16 or wider, within the bound.
A program may use at most 192 MiB of HBM per device.

v0:
```python
import jax
import jax.numpy as jnp
from jax import lax
from jax.sharding import PartitionSpec as P


def over_tokens(first_mat, second_mat):
    return lax.dot_general(
        first_mat, second_mat, (((1,), (1,)), ((), ())), preferred_element_type=jnp.float32
    )


def over_hidden(first_mat, second_mat):
    return lax.dot_general(
        first_mat, second_mat, (((0,), (0,)), ((), ())), preferred_element_type=jnp.float32
    )


def activation_parts(gate_pre, up_pre):
    sig = jax.nn.sigmoid(gate_pre)
    act = gate_pre * sig
    hidden_act = (act * up_pre).astype(jnp.bfloat16)
    return (sig, act, hidden_act)


def pre_grads(hidden_grad, gate_pre, up_pre, sig, act):
    grad_gate_pre = (hidden_grad * up_pre * sig * (1.0 + gate_pre * (1.0 - sig))).astype(
        jnp.bfloat16
    )
    grad_up_pre = (hidden_grad * act).astype(jnp.bfloat16)
    return (grad_gate_pre, grad_up_pre)


def on_device(layer_input, output_grad, gate_weight, up_weight, down_weight):
    block_in = lax.all_gather(layer_input, "row", axis=0, tiled=True)
    gate_pre = jnp.dot(gate_weight, block_in, preferred_element_type=jnp.float32)
    up_pre = jnp.dot(up_weight, block_in, preferred_element_type=jnp.float32)
    sig, act, hidden_act = activation_parts(gate_pre, up_pre)
    block_in = lax.all_gather(output_grad, "row", axis=0, tiled=True)
    grad_new = jnp.dot(down_weight, block_in, preferred_element_type=jnp.float32)
    grad_block = over_tokens(hidden_act, block_in).astype(jnp.bfloat16)
    grad_gate_pre, grad_up_pre = pre_grads(grad_new, gate_pre, up_pre, sig, act)
    block_in = lax.all_gather(layer_input, "row", axis=0, tiled=True)
    gate_grad = over_tokens(grad_gate_pre, block_in).astype(jnp.bfloat16)
    up_grad = over_tokens(grad_up_pre, block_in).astype(jnp.bfloat16)
    terms = over_hidden(gate_weight, grad_gate_pre) + over_hidden(up_weight, grad_up_pre)
    input_grad = lax.psum_scatter(terms, "row", scatter_dimension=0, tiled=True).astype(
        jnp.bfloat16
    )
    return (input_grad, gate_grad, up_grad, grad_block)


def solution(mesh):
    return jax.shard_map(
        on_device,
        mesh=mesh,
        in_specs=(
            P("row", "groups"),
            P("row", "groups"),
            P(("groups", "row"), None),
            P(("groups", "row"), None),
            P(("groups", "row"), None),
        ),
        out_specs=(
            P("row", "groups"),
            P(("groups", "row"), None),
            P(("groups", "row"), None),
            P(("groups", "row"), None),
        ),
        check_vma=False,
    )
```

profile of v0, /device:TPU:0, one launch (start us, length us, event | category | flops | bytes accessed | tf_op | source)
XLA Modules:
  0.0 256.2 jit_solution(9589781873817059000)
XLA Ops:
  7.2 0.0 all-gather.5.cloned.1.call-start
  7.2 0.7 all-gather.5.cloned.1.call-update
  7.9 0.0 all-gather.3.cloned.1.call-start
  7.9 0.7 all-gather.3.cloned.1.call-update
  8.6 0.0 reduce-scatter.2.cloned.1.call-start
  8.7 54.6 %all-gather.5.cloned.1.call-done = bf16[8192,256]{1,0:T(8,128)(2,1)} async-done(((bf16[512,256]{1,0:T(8,128)(2,1)}), bf16[8192,256]{1,0:T(8,128)(2,1)}) %all-gather.5.cloned.1.call-update) | async-done | bytes 4194320 | tf_op jit(solution)/shard_map/all_gather | solution.py:35
  63.3 0.0 copy-start
  63.3 0.0 copy-start.1
  63.3 8.6 %fusion.5 = f32[896,256]{1,0:T(8,128)S(1)} fusion(bf16[896,8192]{1,0:T(8,128)(2,1)} %param.7, bf16[8192,256]{1,0:T(8,128)(2,1)} %all-gather.5.cloned.1.call-done), kind=kOutput, calls=%fused_computation.12 | convolution fusion | flops 3758096384 | bytes 19791872 | tf_op jit(solution)/shard_map/dot_general | solution.py:36
  71.9 2.2 copy-done
  74.1 1.2 copy-done.1
  75.3 3.9 %fusion.4 = f32[896,256]{1,0:T(8,128)S(1)} fusion(bf16[896,8192]{1,0:T(8,128)(2,1)S(1)} %copy-done, bf16[8192,256]{1,0:T(8,128)(2,1)S(1)} %copy-done.1), kind=kOutput, calls=%fused_computation.11 | convolution fusion | flops 3758096384 | bytes 19791872 | tf_op jit(solution)/shard_map/dot_general | solution.py:37
  79.2 35.1 %all-gather.3.cloned.1.call-done = bf16[8192,256]{1,0:T(8,128)(2,1)} async-done(((bf16[512,256]{1,0:T(8,128)(2,1)}), bf16[8192,256]{1,0:T(8,128)(2,1)}) %all-gather.3.cloned.1.call-update) | async-done | bytes 4194320 | tf_op jit(solution)/shard_map/all_gather | solution.py:39
  114.4 10.5 %multiply_convert_fusion.1 = (bf16[896,256]{1,0:T(8,128)(2,1)S(1)}, bf16[896,256]{1,0:T(8,128)(2,1)S(1)}) fusion(f32[896,256]{1,0:T(8,128)S(1)} %fusion.5, f32[896,256]{1,0:T(8,128)S(1)} %fusion.4, bf16[896,8192]{1,0:T(8,128)(2,1)} %param.9, bf16[8192,256]{1,0:T(8,128)(2,1)} %all-gather.3.cloned.1.call-done), kind=kOutput, calls=%fused_computation.6 | convolution fusion | flops 3761078272 | bytes 21626880 | tf_op jit(solution)/shard_map/dot_general | solution.py:40
  124.9 8.0 %fusion.6 = f32[256,8192]{1,0:T(8,128)S(1)} fusion(bf16[896,256]{1,0:T(8,128)(2,1)S(1)} %get-tuple-element.9, bf16[896,8192]{1,0:T(8,128)(2,1)} %param.7), kind=kOutput, calls=%fused_computation.13 | convolution fusion | flops 3758096384 | bytes 23527424 | tf_op jit(solution)/shard_map/dot_general | solution.py:14
  132.9 12.5 %fusion = f32[8192,256]{0,1:T(8,128)} fusion(f32[256,8192]{1,0:T(8,128)S(1)} %fusion.6, bf16[896,256]{1,0:T(8,128)(2,1)S(1)} %get-tuple-element.8, bf16[896,8192]{1,0:T(8,128)(2,1)} %param.8), kind=kOutput, calls=%fused_computation.4 | convolution fusion | flops 3760193536 | bytes 31916032 | tf_op jit(solution)/shard_map/dot_general | solution.py:14
  145.4 0.0 reduce-scatter.2.cloned.1.call-update
  145.5 10.4 %convolution_convert_fusion.1 = bf16[896,8192]{1,0:T(8,128)(2,1)} fusion(bf16[896,256]{1,0:T(8,128)(2,1)S(1)} %get-tuple-element.8, bf16[8192,256]{1,0:T(8,128)(2,1)} %all-gather.5.cloned.1.call-done), kind=kOutput, calls=%fused_computation.1 | convolution fusion | flops 3765436416 | bytes 19333120 | tf_op jit(solution)/shard_map/dot_general | solution.py:8
  155.9 10.6 %convolution_convert_fusion.2 = bf16[896,8192]{1,0:T(8,128)(2,1)} fusion(bf16[896,256]{1,0:T(8,128)(2,1)S(1)} %get-tuple-element.9, bf16[8192,256]{1,0:T(8,128)(2,1)} %all-gather.5.cloned.1.call-done), kind=kOutput, calls=%fused_computation.2 | convolution fusion | flops 3765436416 | bytes 19333120 | tf_op jit(solution)/shard_map/dot_general | solution.py:8
  166.5 9.8 %convolution_convert_fusion = bf16[896,8192]{1,0:T(8,128)(2,1)} fusion(bf16[8192,256]{1,0:T(8,128)(2,1)} %all-gather.3.cloned.1.call-done, f32[896,256]{1,0:T(8,128)S(1)} %fusion.4, f32[896,256]{1,0:T(8,128)S(1)} %fusion.5), kind=kOutput, calls=%fused_computation | convolution fusion | flops 3766812672 | bytes 20709376 | tf_op jit(solution)/shard_map/dot_general | solution.py:8
  176.4 71.4 %reduce-scatter.2.cloned.1.call-done = f32[512,256]{0,1:T(8,128)} async-done(((f32[8192,256]{0,1:T(8,128)}), f32[512,256]{0,1:T(8,128)}) %reduce-scatter.2.cloned.1.call-update) | async-done | bytes 524304 | tf_op jit(solution)/shard_map/reduce_scatter | solution.py:47
  247.8 1.1 convert_element_type.23
  248.9 0.8 copy.9
Async XLA Ops:
  7.2 56.1 %all-gather.5.cloned.1.call-start = ((), (), s32[]{:S(2)}) async-start(), calls=%async_computation.2 | async-start | bytes 4456448 | tf_op jit(solution)/shard_map/all_gather | solution.py:35
  7.9 106.5 %all-gather.3.cloned.1.call-start = ((), (), s32[]{:S(2)}) async-start(), calls=%async_computation.1 | async-start | bytes 4456448 | tf_op jit(solution)/shard_map/all_gather | solution.py:39
  8.6 239.1 %reduce-scatter.2.cloned.1.call-start = ((), (), s32[]{:S(2)}) async-start(), calls=%async_computation.3 | async-start | bytes 8912896 | tf_op jit(solution)/shard_map/reduce_scatter | solution.py:47
  63.3 10.8 %copy-start = (bf16[896,8192]{1,0:T(8,128)(2,1)S(1)}, bf16[896,8192]{1,0:T(8,128)(2,1)}, u32[]{:S(2)}) copy-start(bf16[896,8192]{1,0:T(8,128)(2,1)} %param.8) | copy-start | bytes 44040196
  63.3 12.0 %copy-start.1 = (bf16[8192,256]{1,0:T(8,128)(2,1)S(1)}, bf16[8192,256]{1,0:T(8,128)(2,1)}, u32[]{:S(2)}) copy-start(bf16[8192,256]{1,0:T(8,128)(2,1)} %all-gather.5.cloned.1.call-done) | copy-start | bytes 12582916
Sparse Core Ops, SparseCore 0:
  10.1 53.0 all-gather.4
  65.4 48.8 all-gather.2
  145.6 102.1 reduce-scatter.1
where the time goes:
time: 257 us; the launch traced here: 256 us
  waiting for transfers between devices  163 us (63%)
  matrix products  74.5 us (29%)
  between operations  13.8 us (5%)
  local copies, waits for them, and re-layouts  4.25 us (2%)
    reduce_scatter x1, waiting for transfers between devices, on_device(): lax.psum_scatter(terms, 'row', scatter_dimension=0, tiled=True)  71.4 us
    all_gather x1, waiting for transfers between devices, on_device(): block_in = lax.all_gather(layer_input, 'row', axis=0, tiled=True)  54.6 us
    all_gather x1, waiting for transfers between devices, on_device(): block_in = lax.all_gather(output_grad, 'row', axis=0, tiled=True)  35.1 us
    dot_general x3, matrix products, over_tokens(): lax.dot_general(first_mat, second_mat, (((1,), (1,)), ((), ())), preferre...  30.9 us
    dot_general x2, matrix products, over_hidden(): lax.dot_general(first_mat, second_mat, (((0,), (0,)), ((), ())), preferre...  20.6 us
    dot_general x1, matrix products, on_device(): jnp.dot(down_weight, block_in, preferred_element_type=jnp.float32)  10.5 us
    dot_general x1, matrix products, on_device(): jnp.dot(gate_weight, block_in, preferred_element_type=jnp.float32)  8.59 us
  transfers between devices with their start and end apart: 3, of which 3 were waited for; matrix products, arithmetic and copies ran while one was open for 17% of the time, Pallas kernels for 0%

commit v1 on v0

--- a/solution.py
+++ b/solution.py
@@ -32,7 +32,9 @@
 
 
 def on_device(layer_input, output_grad, gate_weight, up_weight, down_weight):
-    block_in = lax.all_gather(layer_input, "row", axis=0, tiled=True)
+    block_in = jnp.concatenate(
+        lax.all_to_all(jnp.stack([layer_input] * lax.axis_size("row")), "row", 0, 0), axis=0
+    )
     gate_pre = jnp.dot(gate_weight, block_in, preferred_element_type=jnp.float32)
     up_pre = jnp.dot(up_weight, block_in, preferred_element_type=jnp.float32)
     sig, act, hidden_act = activation_parts(gate_pre, up_pre)

time: 257 us -> 307 us (1.19)
  waiting for transfers between devices: 163 us -> 201 us
  starting transfers between devices: 0.11 us -> 7.68 us
  matrix products: 74.5 us -> 77.6 us
    all_to_all x0 -> x1, waiting for transfers between devices: none -> 102 us  [on_device(): lax.all_to_all(jnp.stack([layer_input] * lax.axis_size('row')), 'row', 0, 0)]
    all_gather x1, waiting for transfers between devices: 54.6 us -> 3.47 us  [on_device(): block_in = lax.all_gather(layer_input, 'row', axis=0, tiled=True)]
    all_gather x1, waiting for transfers between devices: 35.1 us -> 0.01 us  [on_device(): block_in = lax.all_gather(output_grad, 'row', axis=0, tiled=True)]
    reduce_scatter x1, waiting for transfers between devices: 71.4 us -> 93.7 us  [on_device(): lax.psum_scatter(terms, 'row', scatter_dimension=0, tiled=True)]
    all_to_all x0 -> x1, starting transfers between devices: none -> 7.57 us  [on_device(): lax.all_to_all(jnp.stack([layer_input] * lax.axis_size('row')), 'row', 0, 0)]
    another operation x0 -> x1, local copies, waits for them, and re-layouts: none -> 3.37 us  [on_device(): jnp.stack([layer_input] * lax.axis_size('row'))]
    dot_general x1, matrix products: 3.94 us -> 7.05 us  [on_device(): up_pre = jnp.dot(up_weight, block_in, preferred_element_type=jnp.float32)]
  transfers between devices with their start and end apart: 3 -> 4, of which waited for: 3 -> 3; matrix products, arithmetic and copies ran while one was open for 17% -> 26% of each run, Pallas kernels for 0% -> 0%
where the time goes in v1:
time: 307 us
  waiting for transfers between devices  201 us (65%)
  matrix products  77.6 us (25%)
  between operations  13.8 us (4%)
  starting transfers between devices  7.68 us (3%)
  local copies, waits for them, and re-layouts  5.9 us (2%)
    all_to_all x1, waiting for transfers between devices, on_device(): lax.all_to_all(jnp.stack([layer_input] * lax.axis_size('row')), 'row', 0, 0)  102 us
    reduce_scatter x1, waiting for transfers between devices, on_device(): lax.psum_scatter(terms, 'row', scatter_dimension=0, tiled=True)  93.7 us
    dot_general x3, matrix products, over_tokens(): lax.dot_general(first_mat, second_mat, (((1,), (1,)), ((), ())), preferre...  29.9 us
    dot_general x2, matrix products, over_hidden(): lax.dot_general(first_mat, second_mat, (((0,), (0,)), ((), ())), preferre...  21.2 us
    dot_general x1, matrix products, on_device(): jnp.dot(down_weight, block_in, preferred_element_type=jnp.float32)  10.8 us
    dot_general x1, matrix products, on_device(): jnp.dot(gate_weight, block_in, preferred_element_type=jnp.float32)  8.6 us
    all_to_all x1, starting transfers between devices, on_device(): lax.all_to_all(jnp.stack([layer_input] * lax.axis_size('row')), 'row', 0, 0)  7.57 us
    dot_general x1, matrix products, on_device(): up_pre = jnp.dot(up_weight, block_in, preferred_element_type=jnp.float32)  7.05 us
  transfers between devices with their start and end apart: 4, of which 3 were waited for; matrix products, arithmetic and copies ran while one was open for 26% of the time, Pallas kernels for 0%

profile of v1, /device:TPU:0, one launch (start us, length us, event | category | flops | bytes accessed | tf_op | source)
XLA Modules:
  0.0 306.6 jit_solution(17568805911509957434)
XLA Ops:
  7.2 0.0 all-gather.3.cloned.1.call-start
  7.2 0.7 all-gather.3.cloned.1.call-update
  7.9 3.4 %stack.2 = bf16[16,512,256]{2,1,0:T(8,128)(2,1)} broadcast(bf16[512,256]{1,0:T(8,128)(2,1)} %param.5), dimensions={1,2} | broadcast | bytes 4456448 | tf_op jit(solution)/shard_map/stack | solution.py:36
  11.3 7.6 %all-to-all-start = ((bf16[16,512,256]{2,1,0:T(8,128)(2,1)}), bf16[16,512,256]{2,1,0:T(8,128)(2,1)}, u32[]{:S(2)}, u32[]{:S(2)}) async-start(bf16[16,512,256]{2,1,0:T(8,128)(2,1)} %stack.2), calls=%async_computation | async-start | bytes 8388608 | tf_op jit(solution)/shard_map/all_to_all | solution.py:36
  18.8 0.0 all-gather.5.cloned.1.call-start
  18.9 0.7 all-gather.5.cloned.1.call-update
  19.6 0.0 reduce-scatter.2.cloned.1.call-start
  19.6 102.0 %all-to-all-done = bf16[16,512,256]{2,1,0:T(8,128)(2,1)} async-done(((bf16[16,512,256]{2,1,0:T(8,128)(2,1)}), bf16[16,512,256]{2,1,0:T(8,128)(2,1)}, u32[]{:S(2)}, u32[]{:S(2)}) %all-to-all-start) | async-done | bytes 4194336 | tf_op jit(solution)/shard_map/all_to_all | solution.py:36
  121.6 8.6 %fusion.5 = f32[896,256]{1,0:T(8,128)S(1)} fusion(bf16[896,8192]{1,0:T(8,128)(2,1)} %param.7, bf16[8192,256]{1,0:T(8,128)(2,1)} %bitcast), kind=kOutput, calls=%fused_computation.12 | convolution fusion | flops 3758096384 | bytes 19791872 | tf_op jit(solution)/shard_map/dot_general | solution.py:38
  130.2 0.0 slice-done
  130.3 0.4 slice-done.2
  130.6 1.3 slice-done.3
  131.9 7.1 %fusion.4 = f32[896,256]{1,0:T(8,128)} fusion(bf16[896,8192]{1,0:T(8,128)(2,1)S(1)} %bitcast.19, bf16[8192,256]{1,0:T(8,128)(2,1)} %bitcast), kind=kOutput, calls=%fused_computation.11 | convolution fusion | flops 3758096384 | bytes 19791872 | tf_op jit(solution)/shard_map/dot_general | solution.py:39
  139.0 10.8 %multiply_convert_fusion.1 = (bf16[896,256]{1,0:T(8,128)(2,1)S(1)}, bf16[896,256]{1,0:T(8,128)(2,1)S(1)}) fusion(f32[896,256]{1,0:T(8,128)S(1)} %fusion.5, f32[896,256]{1,0:T(8,128)} %fusion.4, bf16[896,8192]{1,0:T(8,128)(2,1)} %param.9, bf16[8192,256]{1,0:T(8,128)(2,1)} %all-gather.3.cloned.1.call-done), kind=kOutput, calls=%fused_computation.6 | convolution fusion | flops 3761078272 | bytes 21626880 | tf_op jit(solution)/shard_map/dot_general | solution.py:42
  149.8 8.6 %fusion.6 = f32[256,8192]{1,0:T(8,128)S(1)} fusion(bf16[896,256]{1,0:T(8,128)(2,1)S(1)} %get-tuple-element.9, bf16[896,8192]{1,0:T(8,128)(2,1)} %param.7), kind=kOutput, calls=%fused_computation.13 | convolution fusion | flops 3758096384 | bytes 23527424 | tf_op jit(solution)/shard_map/dot_general | solution.py:14
  158.4 12.6 %fusion = f32[8192,256]{0,1:T(8,128)} fusion(f32[256,8192]{1,0:T(8,128)S(1)} %fusion.6, bf16[896,256]{1,0:T(8,128)(2,1)S(1)} %get-tuple-element.8, bf16[896,8192]{1,0:T(8,128)(2,1)} %param.8), kind=kOutput, calls=%fused_computation.4 | convolution fusion | flops 3760193536 | bytes 31916032 | tf_op jit(solution)/shard_map/dot_general | solution.py:14
  171.0 0.0 reduce-scatter.2.cloned.1.call-update
  171.0 3.5 %all-gather.5.cloned.1.call-done = bf16[8192,256]{1,0:T(8,128)(2,1)} async-done(((bf16[512,256]{1,0:T(8,128)(2,1)}), bf16[8192,256]{1,0:T(8,128)(2,1)}) %all-gather.5.cloned.1.call-update) | async-done | bytes 4194320 | tf_op jit(solution)/shard_map/all_gather | solution.py:45
  174.5 9.8 %convolution_convert_fusion.1 = bf16[896,8192]{1,0:T(8,128)(2,1)} fusion(bf16[896,256]{1,0:T(8,128)(2,1)S(1)} %get-tuple-element.8, bf16[8192,256]{1,0:T(8,128)(2,1)} %all-gather.5.cloned.1.call-done), kind=kOutput, calls=%fused_computation.1 | convolution fusion | flops 3765436416 | bytes 19333120 | tf_op jit(solution)/shard_map/dot_general | solution.py:8
  184.2 9.8 %convolution_convert_fusion.2 = bf16[896,8192]{1,0:T(8,128)(2,1)} fusion(bf16[896,256]{1,0:T(8,128)(2,1)S(1)} %get-tuple-element.9, bf16[8192,256]{1,0:T(8,128)(2,1)} %all-gather.5.cloned.1.call-done), kind=kOutput, calls=%fused_computation.2 | convolution fusion | flops 3765436416 | bytes 19333120 | tf_op jit(solution)/shard_map/dot_general | solution.py:8
  194.1 10.3 %convolution_convert_fusion = bf16[896,8192]{1,0:T(8,128)(2,1)} fusion(bf16[8192,256]{1,0:T(8,128)(2,1)} %all-gather.3.cloned.1.call-done, f32[896,256]{1,0:T(8,128)S(1)} %copy-done, f32[896,256]{1,0:T(8,128)S(1)} %fusion.5), kind=kOutput, calls=%fused_computation | convolution fusion | flops 3766812672 | bytes 20709376 | tf_op jit(solution)/shard_map/dot_general | solution.py:8
  204.4 93.7 %reduce-scatter.2.cloned.1.call-done = f32[512,256]{0,1:T(8,128)} async-done(((f32[8192,256]{0,1:T(8,128)}), f32[512,256]{0,1:T(8,128)}) %reduce-scatter.2.cloned.1.call-update) | async-done | bytes 524304 | tf_op jit(solution)/shard_map/reduce_scatter | solution.py:49
  298.1 1.1 convert_element_type.23
  299.2 0.8 copy.9
  (9 shorter events, 0.0 us)
Async XLA Ops:
  7.2 131.8 %all-gather.3.cloned.1.call-start = ((), (), s32[]{:S(2)}) async-start(), calls=%async_computation.2 | async-start | bytes 4456448 | tf_op jit(solution)/shard_map/all_gather | solution.py:41
  11.3 119.0 %slice-start = ((s8[14680064]{0:T(1024)(128)(4,1)}), s8[2097152]{0:T(1024)(128)(4,1)S(1)}, s32[]{:S(2)}) async-start(s8[14680064]{0:T(1024)(128)(4,1)} %bitcast.18), calls=%async_computation.5 | async-start | bytes 4194304
  11.3 110.4 %all-to-all-start = ((bf16[16,512,256]{2,1,0:T(8,128)(2,1)}), bf16[16,512,256]{2,1,0:T(8,128)(2,1)}, u32[]{:S(2)}, u32[]{:S(2)}) async-start(bf16[16,512,256]{2,1,0:T(8,128)(2,1)} %stack.2), calls=%async_computation | async-start | bytes 8388608 | tf_op jit(solution)/shard_map/all_to_all | solution.py:36
  18.8 155.6 %all-gather.5.cloned.1.call-start = ((), (), s32[]{:S(2)}) async-start(), calls=%async_computation.4 | async-start | bytes 4456448 | tf_op jit(solution)/shard_map/all_gather | solution.py:45
  19.6 278.5 %reduce-scatter.2.cloned.1.call-start = ((), (), s32[]{:S(2)}) async-start(), calls=%async_computation.3 | async-start | bytes 8912896 | tf_op jit(solution)/shard_map/reduce_scatter | solution.py:49
  121.6 8.6 %slice-start.1 = ((s8[14680064]{0:T(1024)(128)(4,1)}), s8[4194304]{0:T(1024)(128)(4,1)S(1)}, s32[]{:S(2)}) async-start(s8[14680064]{0:T(1024)(128)(4,1)} %bitcast.18), calls=%async_computation.6 | async-start | bytes 8388608
  121.6 9.0 %slice-start.2 = ((s8[14680064]{0:T(1024)(128)(4,1)}), s8[4194304]{0:T(1024)(128)(4,1)S(1)}, s32[]{:S(2)}) async-start(s8[14680064]{0:T(1024)(128)(4,1)} %bitcast.18), calls=%async_computation.7 | async-start | bytes 8388608
  121.6 10.3 %slice-start.3 = ((s8[14680064]{0:T(1024)(128)(4,1)}), s8[4194304]{0:T(1024)(128)(4,1)S(1)}, s32[]{:S(2)}) async-start(s8[14680064]{0:T(1024)(128)(4,1)} %bitcast.18), calls=%async_computation.8 | async-start | bytes 8388608
  184.2 9.8 %copy-start = (f32[896,256]{1,0:T(8,128)S(1)}, f32[896,256]{1,0:T(8,128)}, u32[]{:S(2)}) copy-start(f32[896,256]{1,0:T(8,128)} %fusion.4) | copy-start | bytes 2752516
Sparse Core Ops, SparseCore 0:
  10.1 105.3 all-gather.2
  117.6 56.7 all-gather.4
  178.6 119.5 reduce-scatter.1
